TPU v7x, 256 devices: a whole 4x4x8 slice. The times are simulated.
256 devices in a mesh: grp: 8 (over x, core), dev: 32 (over y, z).
Axes of the slice: x: 4, y: 4, z: 8, core: 2. Of those that a mesh axis runs over, the one named last changes fastest.
Arguments:
- queries: bfloat16 [65536, 768], P(('grp', 'dev')), may hold values from -1.796875 to 1.796875
- query_slots: int32 [65536], P('grp'), may hold values from 0 to 8191, as said below
- w_res: bfloat16 [768, 768], replicated, may hold values from -0.21875 to 0.21875
- labels: bfloat16 [5120, 128, 768], P(('grp', 'dev')), may hold values from -0.71875 to 0.71875
- blocks: int32 [512, 12], P('grp'), may hold values from 0 to 5119, as said below
- positives: int32 [65536, 4], P(('grp', 'dev')), may hold values from 0 to 655359, as said below
Outputs:
- query_loss: float32 [65536], P(('grp', 'dev'))
- query_grad: bfloat16 [65536, 768], P(('grp', 'dev'))
- label_grad: bfloat16 [5120, 128, 768], P(('grp', 'dev'))
- residual_grad: bfloat16 [768, 768], replicated
Inputs may be any that keep to these rules, and one draw needn't show every extreme that they name: `query_slots`: the rows of one grp index (rows g * 256 * 32 onward) hold a permutation of 0 to 8191; a place // 256 is the dev index that owns the query's cluster, and the 256 rows of every device send exactly 8 queries to each owner. Row c lists 12 different blocks, all held by devices of the same grp index as the cluster's owner (device c // 2). The 2 clusters of one device list at most 16 distinct blocks, of which at most 1 are held by any one device; for every device's clusters some holder reaches 1. `positives`: the 4 labels of row r are different and lie in 4 different blocks listed for cluster r // 128.
All inputs are finite; a program needn't handle non-finite values.
Results may differ from a plain program's by a relative error of at most 0.0047.
The roundings to bfloat16 on the way count: a program that leaves them out, or rounds other values in their place, can miss the bound.
Values may be sent and summed in bfloat16 or wider, within the bound.
No kernel may reach another device: no remote copies, remote signals or barrier semaphores. Data moves between devices by JAX's collectives and lax.ppermute only.
A program may use at most 128 MiB of HBM per device.

v0:
```python
from functools import partial
import jax
import jax.numpy as jnp
from jax import lax
from jax.sharding import PartitionSpec as P

BLK = 128
CSIZE = 128
SHORT = 12
NPOS = 4
POOL = 16
BLK_DEV = 20


def activate(values):
    return jax.nn.gelu(values, approximate=True)


def activate_slope(values):
    return jax.vjp(activate, values)[1](jnp.ones_like(values))[0]


def request_plan(listed, owner_base, peer_count, per_owner):
    owners = listed // BLK_DEV - owner_base
    within = listed % BLK_DEV
    positions = jnp.arange(listed.shape[0], dtype=jnp.int32)
    earlier = positions[None, :] < positions[:, None]
    same_block = listed[:, None] == listed[None, :]
    leading = jnp.logical_not(jnp.any(same_block & earlier, axis=1))
    first_seen = jnp.argmax(same_block, axis=1)
    same_owner = owners[:, None] == owners[None, :]
    ranking = jnp.sum(same_owner & earlier & leading[None, :], axis=1)
    own_place = owners * per_owner + ranking
    placed = own_place[first_seen]
    target = jnp.where(leading, own_place, peer_count * per_owner)
    request_table = (
        jnp.full((peer_count * per_owner,), -1, jnp.int32).at[target].set(within, mode="drop")
    )
    return (placed, request_table.reshape(peer_count, per_owner))


def local(queries, query_slots, w_res, labels, blocks, positives):
    peer_count = lax.axis_size("dev")
    groups = lax.axis_size("grp")
    own_index = lax.axis_index("dev")
    group_index = lax.axis_index("grp")
    rows_dev = queries.shape[0]
    feature_width = queries.shape[1]
    per_peer = rows_dev // peer_count
    clusters_dev = rows_dev // CSIZE
    per_owner = (POOL + peer_count - 1) // peer_count
    slots_total = peer_count * per_owner
    own_slots = lax.dynamic_slice_in_dim(query_slots, own_index * rows_dev, rows_dev)
    outbound = jnp.argsort(own_slots // rows_dev, stable=True)
    slot_grid = query_slots.reshape(peer_count, rows_dev)
    grid_order = jnp.argsort(slot_grid // rows_dev, axis=1, stable=True)
    grid_sorted = jnp.take_along_axis(slot_grid, grid_order, axis=1)
    incoming = (
        lax.dynamic_slice_in_dim(grid_sorted, own_index * per_peer, per_peer, 1).reshape(rows_dev)
        - own_index * rows_dev
    )
    arrange = jnp.argsort(incoming)
    pre_act = jnp.dot(queries, w_res, preferred_element_type=jnp.float32)
    payload = (queries.astype(jnp.float32) + activate(pre_act)).astype(jnp.bfloat16)
    arrived = lax.all_to_all(
        payload[outbound].reshape(peer_count, per_peer, feature_width),
        "dev",
        split_axis=0,
        concat_axis=0,
        tiled=True,
    )
    arrived = arrived.reshape(rows_dev, feature_width)[arrange]
    listed_all = blocks.reshape(peer_count, clusters_dev * SHORT)
    owner_base = group_index * peer_count
    planner = partial(
        request_plan, owner_base=owner_base, peer_count=peer_count, per_owner=per_owner
    )
    places_all, tables_all = jax.vmap(planner)(listed_all)
    own_places = places_all[own_index].reshape(clusters_dev, SHORT)
    wanted_flat = tables_all[:, own_index, :].reshape(-1)
    block_range = jnp.arange(labels.shape[0], dtype=jnp.int32)
    reply_pick = (wanted_flat[:, None] == block_range[None, :]).astype(jnp.bfloat16)
    reply_blocks = jnp.einsum(
        "sb,bjd->sjd", reply_pick, labels, preferred_element_type=jnp.float32
    ).astype(jnp.bfloat16)
    fetched = lax.all_to_all(
        reply_blocks.reshape(peer_count, per_owner, BLK, feature_width),
        "dev",
        split_axis=0,
        concat_axis=0,
        tiled=True,
    )
    fetched = fetched.reshape(slots_total, BLK, feature_width)
    listed_ids = listed_all[own_index].reshape(clusters_dev, SHORT)
    cluster_rows = arrived.reshape(clusters_dev, CSIZE, feature_width)
    wanted_pos = positives.reshape(clusters_dev, CSIZE, NPOS)
    offsets = jnp.arange(BLK, dtype=jnp.int32)
    slot_range = jnp.arange(slots_total, dtype=jnp.int32)
    place_pick = (own_places[:, :, None] == slot_range[None, None, :]).astype(jnp.bfloat16)

    def per_cluster(running, pieces):
        rows_here, pick_here, ids_here, pos_here = pieces
        chosen = jnp.einsum(
            "ks,sjd->kjd", pick_here, fetched, preferred_element_type=jnp.float32
        ).astype(jnp.bfloat16)
        logits = jnp.einsum("qd,kjd->qkj", rows_here, chosen, preferred_element_type=jnp.float32)
        label_ids = ids_here[:, None] * BLK + offsets[None, :]
        targets = jnp.any(
            label_ids[None, :, :, None] == pos_here[:, None, None, :], axis=-1
        ).astype(jnp.float32)
        loss_rows = jnp.mean(jax.nn.softplus(logits) - targets * logits, axis=(1, 2))
        errors = (jax.nn.sigmoid(logits) - targets).astype(jnp.bfloat16)
        grad_rows = jnp.einsum(
            "qkj,kjd->qd", errors, chosen, preferred_element_type=jnp.float32
        ).astype(jnp.bfloat16)
        terms_cluster = jnp.einsum(
            "qkj,qd->kjd", errors, rows_here, preferred_element_type=jnp.float32
        )
        return (running, (loss_rows, grad_rows, terms_cluster))

    pieces = (cluster_rows, place_pick, listed_ids, wanted_pos)
    running, (losses, grads, terms) = lax.scan(per_cluster, jnp.zeros((), jnp.float32), pieces)
    selector = (own_places.reshape(-1)[:, None] == slot_range[None, :]).astype(jnp.float32)
    summed = jnp.einsum(
        "rs,rjd->sjd",
        selector,
        terms.reshape(-1, BLK, feature_width),
        precision=lax.Precision.HIGHEST,
        preferred_element_type=jnp.float32,
    )
    returned_grads = lax.all_to_all(
        summed.astype(jnp.bfloat16).reshape(peer_count, per_owner, BLK, feature_width),
        "dev",
        split_axis=0,
        concat_axis=0,
        tiled=True,
    )
    returned_grads = returned_grads.reshape(slots_total, BLK, feature_width)
    label_grad = jnp.einsum(
        "sb,sjd->bjd", reply_pick, returned_grads, preferred_element_type=jnp.float32
    ).astype(jnp.bfloat16)
    cluster_grad = grads.reshape(rows_dev, feature_width)
    returned = lax.all_to_all(
        cluster_grad[incoming].reshape(peer_count, per_peer, feature_width),
        "dev",
        split_axis=0,
        concat_axis=0,
        tiled=True,
    )
    restored = returned.reshape(rows_dev, feature_width)[jnp.argsort(outbound)]
    grad_pre = (restored.astype(jnp.float32) * activate_slope(pre_act)).astype(jnp.bfloat16)
    back_term = jnp.einsum("qe,de->qd", grad_pre, w_res, preferred_element_type=jnp.float32)
    query_grad = (restored.astype(jnp.float32) + back_term).astype(jnp.bfloat16)
    weight_term = jnp.einsum("qd,qe->de", queries, grad_pre, preferred_element_type=jnp.float32)
    weight_sum = lax.psum(weight_term, ("grp", "dev"))
    scale_factor = float(rows_dev * peer_count * groups) ** (-0.5)
    return (
        losses.reshape(rows_dev),
        query_grad,
        label_grad,
        (weight_sum * scale_factor).astype(jnp.bfloat16),
    )


def solution(mesh):
    in_specs = (
        P(("grp", "dev"), None),
        P("grp"),
        P(),
        P(("grp", "dev"), None, None),
        P("grp", None),
        P(("grp", "dev"), None),
    )
    out_specs = (P(("grp", "dev")), P(("grp", "dev"), None), P(("grp", "dev"), None, None), P())
    return jax.shard_map(local, mesh=mesh, in_specs=in_specs, out_specs=out_specs, check_vma=False)
```

profile of v0, /device:TPU:2, one launch (start us, length us, event | category | flops | bytes accessed | tf_op | source)
XLA Modules:
  0.0 643.6 jit_solution(3490546229624405968)
XLA Ops:
  7.2 0.9 and_select_fusion
  8.1 3.2 sort.65
  11.2 2.6 add_convert_fusion
  13.8 1.9 gather_fusion
  15.8 11.5 %all-to-all-start = ((bf16[32,8,768]{2,1,0:T(8,128)(2,1)}), bf16[32,8,768]{2,1,0:T(8,128)(2,1)S(1)}, u32[]{:S(2)}, u32[]{:S(2)}) async-start(bf16[32,8,768]{2,1,0:T(8,128)(2,1)} %bitcast), calls=%async_computation | async-start | bytes 786432 | tf_op jit(solution)/shard_map/all_to_all | solution.py:65
  27.3 0.1 copy.100
  27.4 0.1 copy.107
  27.5 0.1 and.80
  27.6 0.1 copy.110
  27.7 0.1 copy.108
  28.1 0.2 fusion.41
  28.4 0.1 reshape.326
  28.5 0.2 convert_reduce_fusion
  28.7 0.1 reshape.324
  28.9 37.8 %scatter_fusion = s32[32,32]{1,0:T(8,128)S(1)} fusion(s32[32,32]{1,0:T(8,128)S(1)} %broadcast_in_dim.65, s32[768]{0:T(1024)S(1)} %reshape.324, s32[768]{0:T(1024)S(1)} %reshape.326), kind=kCustom, calls=%fused_computation.6 | custom fusion | bytes 15360 | tf_op jit(solution)/shard_map/vmap()/scatter | solution.py:37
  66.7 0.2 dynamic-slice_reduce_fusion
  66.9 5.4 convert_bitcast_fusion.1
  72.3 6.3 copy.115
  78.5 10.0 %all-to-all-start.1 = ((bf16[32,1,128,768]{3,2,1,0:T(8,128)(2,1)}), bf16[32,1,128,768]{3,2,1,0:T(8,128)(2,1)}, u32[]{:S(2)}, u32[]{:S(2)}) async-start(bf16[32,1,128,768]{3,2,1,0:T(8,128)(2,1)} %copy.115), calls=%async_computation.1 | async-start | bytes 12582912 | tf_op jit(solution)/shard_map/all_to_all | solution.py:86
  88.7 0.6 add_select_fusion
  89.3 0.6 iota.54
  90.0 1.3 compare_reduce_fusion.1
  91.3 0.1 reshape.318
  91.4 5.3 gather_fusion.5
  96.8 0.1 eq.96
  97.1 0.8 fusion.43
  97.9 65.0 %gather_fusion.4 = s32[8192]{0:T(1024)S(1)} fusion(s32[32,256]{1,0:T(8,128)S(1)} %reshape.266, s32[8192]{0:T(1024)S(1)} %bitcast.111), kind=kCustom, calls=%fused_computation.4 | custom fusion | bytes 131072 | tf_op jit(solution)/shard_map/jit(take_along_axis)/gather | solution.py:57
  163.0 0.1 fusion.45
  163.1 0.1 sub.83
  163.2 0.1 sub.76
  163.3 3.2 sort.67
  166.5 1.2 gather_fusion.1
  167.7 60.9 %all-to-all-done.1 = bf16[32,1,128,768]{3,2,1,0:T(8,128)(2,1)} async-done(((bf16[32,1,128,768]{3,2,1,0:T(8,128)(2,1)}), bf16[32,1,128,768]{3,2,1,0:T(8,128)(2,1)}, u32[]{:S(2)}, u32[]{:S(2)}) %all-to-all-start.1) | async-done | bytes 6291488 | tf_op jit(solution)/shard_map/all_to_all | solution.py:86
  228.5 9.0 %copy.116 = bf16[32,128,768]{2,0,1:T(8,128)(2,1)} copy(bf16[32,128,768]{2,1,0:T(8,128)(2,1)} %bitcast.9) | data formatting | bytes 12582912
  237.5 22.7 %while.15 = (s32[]{:T(128)}, f32[2,128]{1,0:T(2,128)S(1)}, bf16[2,128,768]{2,1,0:T(8,128)(2,1)S(1)}, f32[2,12,128,768]{3,2,1,0:T(8,128)}, bf16[2,128,768]{2,1,0:...) while((s32[]{:T(128)}, f32[2,128]{1,0:T(2,128)S(1)}, ...), condition=%wide.region_10.11_spmd.clone, body=%wide.region_7.10_spmd.clone.sunk | while | flops 988628480 | bytes 24667932 | solution.py:122
  237.6 0.5 compare_reduce_fusion.3
  238.1 0.3 copy.148
  238.4 3.8 fusion.90
  242.2 1.5 fusion.91
  243.7 1.6 fusion.92
  245.3 0.6 subtract_reduce_fusion.2
  245.9 2.9 bitcast_dynamic-update-slice_fusion.2
  248.9 0.5 compare_reduce_fusion.3
  249.4 0.3 copy.148
  249.7 3.8 fusion.90
  253.5 1.5 fusion.91
  255.0 1.6 fusion.92
  256.6 0.6 subtract_reduce_fusion.2
  257.2 2.9 bitcast_dynamic-update-slice_fusion.2
  260.2 1.9 gather_fusion.2
  262.1 8.2 %all-to-all-start.2 = ((bf16[32,8,768]{2,1,0:T(8,128)(2,1)}), bf16[32,8,768]{2,1,0:T(8,128)(2,1)S(1)}, u32[]{:S(2)}, u32[]{:S(2)}) async-start(bf16[32,8,768]{2,1,0:T(8,128)(2,1)} %bitcast.14), calls=%async_computation.2 | async-start | bytes 786432 | tf_op jit(solution)/shard_map/all_to_all | solution.py:143
  270.3 14.7 %convert_bitcast_fusion = bf16[32,1,128,768]{3,0,2,1:T(8,128)(2,1)S(1)} fusion(f32[24,128,768]{2,1,0:T(8,128)} %bitcast.115, s32[24]{0:T(128)S(1)} %get-tuple-element.171), kind=kOutput, calls=%fused_computation.42 | convolution fusion | flops 909116160 | bytes 15728736 | tf_op jit(solution)/shard_map/rs,rjd->sjd/dot_general | solution.py:124
  285.0 6.2 copy.118
  291.3 10.2 %all-to-all-start.3 = ((bf16[32,1,128,768]{3,2,1,0:T(8,128)(2,1)}), bf16[32,1,128,768]{3,2,1,0:T(8,128)(2,1)}, u32[]{:S(2)}, u32[]{:S(2)}) async-start(bf16[32,1,128,768]{3,2,1,0:T(8,128)(2,1)} %copy.118), calls=%async_computation.3 | async-start | bytes 12582912 | tf_op jit(solution)/shard_map/all_to_all | solution.py:131
  301.4 0.3 all-reduce.2.cloned.1.call-start
  301.7 3.2 sort.68
  304.9 1.2 gather_fusion.3
  306.1 2.4 convolution_bitcast_fusion.1
  308.5 1.6 fusion.33
  310.1 312.4 %all-reduce.2.cloned.1.call-done = f32[768,768]{0,1:T(8,128)} async-done(((f32[768,768]{0,1:T(8,128)}), f32[768,768]{0,1:T(8,128)}) %all-reduce.2.cloned.1.call-update) | async-done | bytes 2359312 | tf_op jit(solution)/shard_map/psum | solution.py:155
  622.6 1.8 multiply_convert_fusion
  624.4 1.5 copy.121
  625.9 7.9 %fusion.30 = bf16[20,128,768]{2,0,1:T(8,128)(2,1)S(1)} fusion(bf16[32,1,128,768]{3,2,1,0:T(8,128)(2,1)} %all-to-all-done.3, s32[32]{0:T(128)S(1)} %dynamic-slice_reduce_fusion), kind=kOutput, calls=%fused_computation.46 | convolution fusion | flops 127795840 | bytes 10223744 | tf_op jit(solution)/shard_map/sb,sjd->bjd/dot_general | solution.py:139
  633.8 2.8 copy.120
  (72 shorter events, 1.4 us)
Async XLA Ops:
  7.2 4.1 copy-start
  7.2 20.1 %copy-start.2 = (s32[64,12]{0,1:T(8,128)S(1)}, s32[64,12]{0,1:T(8,128)}, u32[]{:S(2)}) copy-start(s32[64,12]{0,1:T(8,128)} %param.12) | copy-start | bytes 9220
  15.8 62.8 %all-to-all-start = ((bf16[32,8,768]{2,1,0:T(8,128)(2,1)}), bf16[32,8,768]{2,1,0:T(8,128)(2,1)S(1)}, u32[]{:S(2)}, u32[]{:S(2)}) async-start(bf16[32,8,768]{2,1,0:T(8,128)(2,1)} %bitcast), calls=%async_computation | async-start | bytes 786432 | tf_op jit(solution)/shard_map/all_to_all | solution.py:65
  78.5 10.1 %copy-start.3 = (s32[8192]{0:T(1024)S(1)}, s32[8192]{0:T(1024)}, u32[]{:S(2)}) copy-start(s32[8192]{0:T(1024)} %param.9) | copy-start | bytes 98308
  78.5 150.0 %all-to-all-start.1 = ((bf16[32,1,128,768]{3,2,1,0:T(8,128)(2,1)}), bf16[32,1,128,768]{3,2,1,0:T(8,128)(2,1)}, u32[]{:S(2)}, u32[]{:S(2)}) async-start(bf16[32,1,128,768]{3,2,1,0:T(8,128)(2,1)} %copy.115), calls=%async_computation.1 | async-start | bytes 12582912 | tf_op jit(solution)/shard_map/all_to_all | solution.py:86
  88.6 8.5 %sort.70.cloned.1.call-start = ((), (), s32[]{:S(2)}) async-start(), calls=%async_computation.5 | async-start | bytes 196640 | tf_op jit(solution)/shard_map/jit(argsort)/sort | solution.py:56
  97.9 65.0 %copy-start.1 = (s32[32,256]{1,0:T(8,128)S(1)}, s32[32,256]{1,0:T(8,128)}, u32[]{:S(2)}) copy-start(s32[32,256]{1,0:T(8,128)} %get-tuple-element.64) | copy-start | bytes 98308
  228.5 9.0 %copy-start.4 = (s32[256,4]{0,1:T(4,128)S(1)}, s32[256,4]{0,1:T(4,128)}, u32[]{:S(2)}) copy-start(s32[256,4]{0,1:T(4,128)} %param.13) | copy-start | bytes 12292
  260.2 24.9 %copy-start.6 = (f32[2,128]{1,0:T(2,128)}, f32[2,128]{1,0:T(2,128)S(1)}, u32[]{:S(2)}) copy-start(f32[2,128]{1,0:T(2,128)S(1)} %get-tuple-element.67) | copy-start | bytes 3076
  262.1 29.2 %all-to-all-start.2 = ((bf16[32,8,768]{2,1,0:T(8,128)(2,1)}), bf16[32,8,768]{2,1,0:T(8,128)(2,1)S(1)}, u32[]{:S(2)}, u32[]{:S(2)}) async-start(bf16[32,8,768]{2,1,0:T(8,128)(2,1)} %bitcast.14), calls=%async_computation.2 | async-start | bytes 786432 | tf_op jit(solution)/shard_map/all_to_all | solution.py:143
  291.3 14.8 %copy-start.5 = (bf16[256,768]{1,0:T(8,128)(2,1)S(1)}, bf16[256,768]{1,0:T(8,128)(2,1)}, u32[]{:S(2)}) copy-start(bf16[256,768]{1,0:T(8,128)(2,1)} %param.8) | copy-start | bytes 1179652
  291.3 14.8 %copy-start.7 = (f32[256,768]{1,0:T(8,128)S(1)}, f32[256,768]{1,0:T(8,128)}, u32[]{:S(2)}) copy-start(f32[256,768]{1,0:T(8,128)} %get-tuple-element.176) | copy-start | bytes 2359300
  291.3 334.6 %all-to-all-start.3 = ((bf16[32,1,128,768]{3,2,1,0:T(8,128)(2,1)}), bf16[32,1,128,768]{3,2,1,0:T(8,128)(2,1)}, u32[]{:S(2)}, u32[]{:S(2)}) async-start(bf16[32,1,128,768]{3,2,1,0:T(8,128)(2,1)} %copy.118), calls=%async_computation.3 | async-start | bytes 12582912 | tf_op jit(solution)/shard_map/all_to_all | solution.py:131
  301.4 321.1 %all-reduce.2.cloned.1.call-start = ((), (), s32[]{:S(2)}) async-start(), calls=%async_computation.4 | async-start | bytes 4718592 | tf_op jit(solution)/shard_map/psum | solution.py:155
Sparse Core Ops, SparseCore 0:
  92.3 2.5 sort.72.cloned.1.call-done
  308.6 313.9 all-reduce.1
  (1 shorter events, 0.0 us)
where the time goes:
time: 652 us; the launch traced here: 644 us
  waiting for transfers between devices  373 us (57%)
  local copies, waits for them, and re-layouts  143 us (22%)
  matrix products  54.2 us (8%)
  starting transfers between devices  40.1 us (6%)
  other arithmetic  17.9 us (3%)
  between operations  14.6 us (2%)
    psum x1, waiting for transfers between devices, local(): weight_sum = lax.psum(weight_term, ('grp', 'dev'))  312 us
    gather x2, local copies, waits for them, and re-layouts, local(): grid_sorted = jnp.take_along_axis(slot_grid, grid_order, axis=1)  65 us
    all_to_all x1, waiting for transfers between devices, local(): lax.all_to_all(reply_blocks.reshape(peer_count, per_owner, BLK, feature_w...  60.9 us
    scatter x3, local copies, waits for them, and re-layouts, request_plan(): jnp.full((peer_count * per_owner,), -1, jnp.int32).at[target]  38 us
    dot_general x1, matrix products, local(): jnp.einsum('rs,rjd->sjd', selector, terms.reshape(-1, BLK, feature_width)...  14.7 us
    unnamed x22, local copies, waits for them, and re-layouts  13.4 us
  transfers between devices with their start and end apart: 5, of which 2 were waited for; matrix products, arithmetic and copies ran while one was open for 25% of the time, Pallas kernels for 0%

commit v1 on v0

--- a/solution.py
+++ b/solution.py
@@ -152,7 +152,7 @@
     back_term = jnp.einsum("qe,de->qd", grad_pre, w_res, preferred_element_type=jnp.float32)
     query_grad = (restored.astype(jnp.float32) + back_term).astype(jnp.bfloat16)
     weight_term = jnp.einsum("qd,qe->de", queries, grad_pre, preferred_element_type=jnp.float32)
-    weight_sum = lax.psum(weight_term, ("grp", "dev"))
+    weight_sum = lax.psum(lax.psum(weight_term, "dev"), "grp")
     scale_factor = float(rows_dev * peer_count * groups) ** (-0.5)
     return (
         losses.reshape(rows_dev),

time: 652 us -> 628 us (0.963)
  waiting for transfers between devices: 373 us -> 347 us
    psum x1 -> x2, waiting for transfers between devices: 312 us -> 286 us  [local(): weight_sum = lax.psum(lax.psum(weight_term, 'dev'), 'grp')]
  transfers between devices with their start and end apart: 5 -> 6, of which waited for: 2 -> 3; matrix products, arithmetic and copies ran while one was open for 25% -> 26% of each run, Pallas kernels for 0% -> 0%
where the time goes in v1:
time: 628 us; the launch traced here: 617 us
  waiting for transfers between devices  347 us (55%)
  local copies, waits for them, and re-layouts  143 us (23%)
  matrix products  54.2 us (9%)
  starting transfers between devices  40.2 us (6%)
  other arithmetic  17.9 us (3%)
  between operations  14.3 us (2%)
    psum x2, waiting for transfers between devices, local(): weight_sum = lax.psum(lax.psum(weight_term, 'dev'), 'grp')  286 us
    gather x2, local copies, waits for them, and re-layouts, local(): grid_sorted = jnp.take_along_axis(slot_grid, grid_order, axis=1)  65 us
    all_to_all x1, waiting for transfers between devices, local(): lax.all_to_all(reply_blocks.reshape(peer_count, per_owner, BLK, feature_w...  60.9 us
    scatter x3, local copies, waits for them, and re-layouts, request_plan(): jnp.full((peer_count * per_owner,), -1, jnp.int32).at[target]  38 us
    dot_general x1, matrix products, local(): jnp.einsum('rs,rjd->sjd', selector, terms.reshape(-1, BLK, feature_width)...  14.7 us
    unnamed x22, local copies, waits for them, and re-layouts  13.4 us
  transfers between devices with their start and end apart: 6, of which 3 were waited for; matrix products, arithmetic and copies ran while one was open for 26% of the time, Pallas kernels for 0%

profile of v1, /device:TPU:2, one launch (start us, length us, event | category | flops | bytes accessed | tf_op | source)
XLA Modules:
  0.0 616.9 jit_solution(13595869501494977813)
XLA Ops:
  7.2 0.9 and_select_fusion
  8.1 3.2 sort.65
  11.2 2.6 add_convert_fusion
  13.8 1.9 gather_fusion
  15.8 11.5 %all-to-all-start = ((bf16[32,8,768]{2,1,0:T(8,128)(2,1)}), bf16[32,8,768]{2,1,0:T(8,128)(2,1)S(1)}, u32[]{:S(2)}, u32[]{:S(2)}) async-start(bf16[32,8,768]{2,1,0:T(8,128)(2,1)} %bitcast), calls=%async_computation | async-start | bytes 786432 | tf_op jit(solution)/shard_map/all_to_all | solution.py:65
  27.3 0.1 copy.100
  27.4 0.1 copy.107
  27.5 0.1 and.80
  27.6 0.1 copy.110
  27.7 0.1 copy.108
  28.1 0.2 fusion.41
  28.4 0.1 reshape.326
  28.5 0.2 convert_reduce_fusion
  28.7 0.1 reshape.324
  28.9 37.8 %scatter_fusion = s32[32,32]{1,0:T(8,128)S(1)} fusion(s32[32,32]{1,0:T(8,128)S(1)} %broadcast_in_dim.65, s32[768]{0:T(1024)S(1)} %reshape.324, s32[768]{0:T(1024)S(1)} %reshape.326), kind=kCustom, calls=%fused_computation.6 | custom fusion | bytes 15360 | tf_op jit(solution)/shard_map/vmap()/scatter | solution.py:37
  66.7 0.2 dynamic-slice_reduce_fusion
  66.9 5.4 convert_bitcast_fusion.1
  72.3 6.3 %copy.115 = bf16[32,1,128,768]{3,2,1,0:T(8,128)(2,1)} copy(bf16[32,1,128,768]{3,0,2,1:T(8,128)(2,1)S(1)} %convert_bitcast_fusion.1) | data formatting | bytes 12582912 | tf_op jit(solution)/shard_map/reshape | solution.py:87
  78.5 10.0 %all-to-all-start.1 = ((bf16[32,1,128,768]{3,2,1,0:T(8,128)(2,1)}), bf16[32,1,128,768]{3,2,1,0:T(8,128)(2,1)}, u32[]{:S(2)}, u32[]{:S(2)}) async-start(bf16[32,1,128,768]{3,2,1,0:T(8,128)(2,1)} %copy.115), calls=%async_computation.1 | async-start | bytes 12582912 | tf_op jit(solution)/shard_map/all_to_all | solution.py:86
  88.7 0.6 add_select_fusion
  89.3 0.6 iota.54
  90.0 1.3 compare_reduce_fusion.1
  91.3 0.1 reshape.318
  91.4 5.3 gather_fusion.5
  97.1 0.8 fusion.43
  97.9 65.0 %gather_fusion.4 = s32[8192]{0:T(1024)S(1)} fusion(s32[32,256]{1,0:T(8,128)S(1)} %reshape.266, s32[8192]{0:T(1024)S(1)} %bitcast.111), kind=kCustom, calls=%fused_computation.4 | custom fusion | bytes 131072 | tf_op jit(solution)/shard_map/jit(take_along_axis)/gather | solution.py:57
  163.0 0.1 fusion.45
  163.1 0.1 sub.83
  163.2 0.1 sub.76
  163.3 3.2 sort.67
  166.5 1.2 gather_fusion.1
  167.7 60.9 %all-to-all-done.1 = bf16[32,1,128,768]{3,2,1,0:T(8,128)(2,1)} async-done(((bf16[32,1,128,768]{3,2,1,0:T(8,128)(2,1)}), bf16[32,1,128,768]{3,2,1,0:T(8,128)(2,1)}, u32[]{:S(2)}, u32[]{:S(2)}) %all-to-all-start.1) | async-done | bytes 6291488 | tf_op jit(solution)/shard_map/all_to_all | solution.py:86
  228.5 9.0 %copy.116 = bf16[32,128,768]{2,0,1:T(8,128)(2,1)} copy(bf16[32,128,768]{2,1,0:T(8,128)(2,1)} %bitcast.9) | data formatting | bytes 12582912
  237.5 22.7 %while.15 = (s32[]{:T(128)}, f32[2,128]{1,0:T(2,128)S(1)}, bf16[2,128,768]{2,1,0:T(8,128)(2,1)S(1)}, f32[2,12,128,768]{3,2,1,0:T(8,128)}, bf16[2,128,768]{2,1,0:...) while((s32[]{:T(128)}, f32[2,128]{1,0:T(2,128)S(1)}, ...), condition=%wide.region_10.11_spmd.clone, body=%wide.region_7.10_spmd.clone.sunk | while | flops 988628480 | bytes 24667932 | solution.py:122
  237.6 0.5 compare_reduce_fusion.3
  238.1 0.3 copy.148
  238.4 3.8 fusion.90
  242.2 1.5 fusion.91
  243.7 1.6 fusion.92
  245.3 0.6 subtract_reduce_fusion.2
  245.9 2.9 bitcast_dynamic-update-slice_fusion.2
  248.9 0.5 compare_reduce_fusion.3
  249.4 0.3 copy.148
  249.7 3.8 fusion.90
  253.5 1.5 fusion.91
  255.0 1.6 fusion.92
  256.6 0.6 subtract_reduce_fusion.2
  257.2 2.9 bitcast_dynamic-update-slice_fusion.2
  260.2 1.9 gather_fusion.2
  262.1 8.2 %all-to-all-start.2 = ((bf16[32,8,768]{2,1,0:T(8,128)(2,1)}), bf16[32,8,768]{2,1,0:T(8,128)(2,1)S(1)}, u32[]{:S(2)}, u32[]{:S(2)}) async-start(bf16[32,8,768]{2,1,0:T(8,128)(2,1)} %bitcast.14), calls=%async_computation.2 | async-start | bytes 786432 | tf_op jit(solution)/shard_map/all_to_all | solution.py:143
  270.3 14.7 %convert_bitcast_fusion = bf16[32,1,128,768]{3,0,2,1:T(8,128)(2,1)S(1)} fusion(f32[24,128,768]{2,1,0:T(8,128)} %bitcast.115, s32[24]{0:T(128)S(1)} %get-tuple-element.171), kind=kOutput, calls=%fused_computation.42 | convolution fusion | flops 909116160 | bytes 15728736 | tf_op jit(solution)/shard_map/rs,rjd->sjd/dot_general | solution.py:124
  285.0 6.2 %copy.118 = bf16[32,1,128,768]{3,2,1,0:T(8,128)(2,1)} copy(bf16[32,1,128,768]{3,0,2,1:T(8,128)(2,1)S(1)} %convert_bitcast_fusion) | data formatting | bytes 12582912 | tf_op jit(solution)/shard_map/reshape | solution.py:132
  291.3 10.2 %all-to-all-start.3 = ((bf16[32,1,128,768]{3,2,1,0:T(8,128)(2,1)}), bf16[32,1,128,768]{3,2,1,0:T(8,128)(2,1)}, u32[]{:S(2)}, u32[]{:S(2)}) async-start(bf16[32,1,128,768]{3,2,1,0:T(8,128)(2,1)} %copy.118), calls=%async_computation.3 | async-start | bytes 12582912 | tf_op jit(solution)/shard_map/all_to_all | solution.py:131
  301.4 0.3 all-reduce.3.cloned.1.call-start
  301.7 3.2 sort.68
  304.9 1.2 gather_fusion.3
  306.1 2.4 convolution_bitcast_fusion.1
  308.5 218.2 %all-reduce.3.cloned.1.call-done = f32[768,768]{0,1:T(8,128)} async-done(((f32[768,768]{0,1:T(8,128)}), f32[768,768]{0,1:T(8,128)}) %all-reduce.3.cloned.1.call-update) | async-done | bytes 2359312 | tf_op jit(solution)/shard_map/psum | solution.py:155
  526.8 1.6 fusion.33
  528.4 67.8 %all-reduce.5.cloned.1.call-done = f32[768,768]{0,1:T(8,128)} async-done(((f32[768,768]{0,1:T(8,128)}), f32[768,768]{0,1:T(8,128)}) %all-reduce.5.cloned.1.call-update) | async-done | bytes 2359312 | tf_op jit(solution)/shard_map/psum | solution.py:155
  596.2 1.8 multiply_convert_fusion
  598.0 1.5 copy.121
  599.5 7.9 %fusion.30 = bf16[20,128,768]{2,0,1:T(8,128)(2,1)S(1)} fusion(bf16[32,1,128,768]{3,2,1,0:T(8,128)(2,1)} %all-to-all-done.3, s32[32]{0:T(128)S(1)} %dynamic-slice_reduce_fusion), kind=kOutput, calls=%fused_computation.46 | convolution fusion | flops 127795840 | bytes 10223744 | tf_op jit(solution)/shard_map/sb,sjd->bjd/dot_general | solution.py:139
  607.4 2.8 copy.120
  (75 shorter events, 1.5 us)
Async XLA Ops:
  7.2 4.1 copy-start
  7.2 20.1 %copy-start.2 = (s32[64,12]{0,1:T(8,128)S(1)}, s32[64,12]{0,1:T(8,128)}, u32[]{:S(2)}) copy-start(s32[64,12]{0,1:T(8,128)} %param.12) | copy-start | bytes 9220
  15.8 62.8 %all-to-all-start = ((bf16[32,8,768]{2,1,0:T(8,128)(2,1)}), bf16[32,8,768]{2,1,0:T(8,128)(2,1)S(1)}, u32[]{:S(2)}, u32[]{:S(2)}) async-start(bf16[32,8,768]{2,1,0:T(8,128)(2,1)} %bitcast), calls=%async_computation | async-start | bytes 786432 | tf_op jit(solution)/shard_map/all_to_all | solution.py:65
  78.5 10.1 %copy-start.3 = (s32[8192]{0:T(1024)S(1)}, s32[8192]{0:T(1024)}, u32[]{:S(2)}) copy-start(s32[8192]{0:T(1024)} %param.9) | copy-start | bytes 98308
  78.5 150.0 %all-to-all-start.1 = ((bf16[32,1,128,768]{3,2,1,0:T(8,128)(2,1)}), bf16[32,1,128,768]{3,2,1,0:T(8,128)(2,1)}, u32[]{:S(2)}, u32[]{:S(2)}) async-start(bf16[32,1,128,768]{3,2,1,0:T(8,128)(2,1)} %copy.115), calls=%async_computation.1 | async-start | bytes 12582912 | tf_op jit(solution)/shard_map/all_to_all | solution.py:86
  88.6 8.5 %sort.70.cloned.1.call-start = ((), (), s32[]{:S(2)}) async-start(), calls=%async_computation.6 | async-start | bytes 196640 | tf_op jit(solution)/shard_map/jit(argsort)/sort | solution.py:56
  97.9 65.0 %copy-start.1 = (s32[32,256]{1,0:T(8,128)S(1)}, s32[32,256]{1,0:T(8,128)}, u32[]{:S(2)}) copy-start(s32[32,256]{1,0:T(8,128)} %get-tuple-element.64) | copy-start | bytes 98308
  228.5 9.0 %copy-start.4 = (s32[256,4]{0,1:T(4,128)S(1)}, s32[256,4]{0,1:T(4,128)}, u32[]{:S(2)}) copy-start(s32[256,4]{0,1:T(4,128)} %param.13) | copy-start | bytes 12292
  260.2 24.9 %copy-start.6 = (f32[2,128]{1,0:T(2,128)}, f32[2,128]{1,0:T(2,128)S(1)}, u32[]{:S(2)}) copy-start(f32[2,128]{1,0:T(2,128)S(1)} %get-tuple-element.67) | copy-start | bytes 3076
  262.1 29.2 %all-to-all-start.2 = ((bf16[32,8,768]{2,1,0:T(8,128)(2,1)}), bf16[32,8,768]{2,1,0:T(8,128)(2,1)S(1)}, u32[]{:S(2)}, u32[]{:S(2)}) async-start(bf16[32,8,768]{2,1,0:T(8,128)(2,1)} %bitcast.14), calls=%async_computation.2 | async-start | bytes 786432 | tf_op jit(solution)/shard_map/all_to_all | solution.py:143
  291.3 14.8 %copy-start.5 = (bf16[256,768]{1,0:T(8,128)(2,1)S(1)}, bf16[256,768]{1,0:T(8,128)(2,1)}, u32[]{:S(2)}) copy-start(bf16[256,768]{1,0:T(8,128)(2,1)} %param.8) | copy-start | bytes 1179652
  291.3 14.8 %copy-start.7 = (f32[256,768]{1,0:T(8,128)S(1)}, f32[256,768]{1,0:T(8,128)}, u32[]{:S(2)}) copy-start(f32[256,768]{1,0:T(8,128)} %get-tuple-element.176) | copy-start | bytes 2359300
  291.3 308.2 %all-to-all-start.3 = ((bf16[32,1,128,768]{3,2,1,0:T(8,128)(2,1)}), bf16[32,1,128,768]{3,2,1,0:T(8,128)(2,1)}, u32[]{:S(2)}, u32[]{:S(2)}) async-start(bf16[32,1,128,768]{3,2,1,0:T(8,128)(2,1)} %copy.118), calls=%async_computation.3 | async-start | bytes 12582912 | tf_op jit(solution)/shard_map/all_to_all | solution.py:131
  301.4 225.3 %all-reduce.3.cloned.1.call-start = ((), (), s32[]{:S(2)}) async-start(), calls=%async_computation.4 | async-start | bytes 4718592 | tf_op jit(solution)/shard_map/psum | solution.py:155
  308.5 287.7 %all-reduce.5.cloned.1.call-start = ((), (), s32[]{:S(2)}) async-start(), calls=%async_computation.5 | async-start | bytes 4718592 | tf_op jit(solution)/shard_map/psum | solution.py:155
Sparse Core Ops, SparseCore 0:
  92.3 2.5 sort.72.cloned.1.call-done
  308.6 218.1 all-reduce.2
  529.2 66.9 all-reduce.4
  (1 shorter events, 0.0 us)
